TPU v7x, 256 devices: a whole 4x4x8 slice. The times are simulated.
256 devices in a mesh: au: 32 (over y, x, core), ia: 8 (over z).
Axes of the slice: x: 4, y: 4, z: 8, core: 2. Of those that a mesh axis runs over, the one named last changes fastest.
Arguments:
- user_emb: float32 [131072, 128], P(('au', 'ia')), may hold values from -6 to 6
- item_emb: float32 [32768, 128], P(('ia', 'au')), may hold values from -6 to 6
- user_degree: int32 [131072], P(('au', 'ia')), may hold values from 1 to 64
- item_degree: int32 [32768], P(('ia', 'au')), may hold values from 1 to 64
- tiles: float32 [32768, 128, 128], P(('au', 'ia')), as said below
- tile_user_block: int32 [32768], P(('au', 'ia')), may hold values from 0 to 31
- tile_item_block: int32 [32768], P(('au', 'ia')), may hold values from 0 to 31
- live_tiles: int32 [256], P(('au', 'ia')), may hold values from 32 to 128, as said below
Outputs:
- user_final: float32 [131072, 128], P(('au', 'ia'))
- item_final: float32 [32768, 128], P(('ia', 'au'))
Inputs may be any that keep to these rules, and one draw needn't show every extreme that they name: Tile slots of grid cell c beyond the first live_tiles[c] are unused; some cell uses all 128. `tiles`: each tile holds weights of 0 or between 0.05 and 0.35.
All inputs are finite; a program needn't handle non-finite values.
Results may differ from a plain program's by a relative error of at most 0.0001.
Values sent between devices are 32-bit elements; how exact they have to be, the bound alone decides.
A program may use at most 128 MiB of HBM per device.

v0:
```python
import jax
import jax.numpy as jnp
from jax import lax
from jax.sharding import PartitionSpec as P

LAYERS = 2


def per_device(
    user_emb,
    item_emb,
    user_degree,
    item_degree,
    tiles,
    tile_user_block,
    tile_item_block,
    live_tiles,
):
    tile_size = tiles.shape[1]
    emb_width = user_emb.shape[1]
    tile_count = tiles.shape[0]
    user_count = user_emb.shape[0]
    user_blocks = user_count * lax.axis_size("ia") // tile_size
    item_blocks = item_emb.shape[0] * lax.axis_size("au") // tile_size
    live_mask = (jnp.arange(tile_count, dtype=jnp.int32) < live_tiles[0]).astype(jnp.float32)
    user_pick = (
        tile_user_block[None, :] == jnp.arange(user_blocks, dtype=jnp.int32)[:, None]
    ).astype(jnp.float32) * live_mask[None, :]
    item_pick = (
        tile_item_block[None, :] == jnp.arange(item_blocks, dtype=jnp.int32)[:, None]
    ).astype(jnp.float32) * live_mask[None, :]
    norm_user = lax.rsqrt(user_degree.astype(jnp.float32))[:, None]
    norm_item = lax.rsqrt(item_degree.astype(jnp.float32))[:, None]
    gathered_users = lax.all_gather(user_emb * norm_user, "ia", axis=0, tiled=True)
    users_now, items_now = (user_emb, item_emb)
    user_total, item_total = (user_emb, item_emb)
    for layer_index in range(LAYERS):
        gathered_items = lax.all_gather(items_now * norm_item, "au", axis=0, tiled=True)
        toward_picked = gathered_items.reshape(item_blocks, tile_size, emb_width)[tile_item_block]
        toward_products = jnp.einsum(
            "tuk,tkd->tud", tiles, toward_picked, precision=lax.Precision.HIGHEST
        )
        toward_summed = jnp.dot(
            user_pick, toward_products.reshape(tile_count, -1), precision=lax.Precision.HIGHEST
        )
        partial_users = toward_summed.reshape(user_blocks * tile_size, emb_width)
        picked = gathered_users.reshape(user_blocks, tile_size, emb_width)[tile_user_block]
        products = jnp.einsum("tuk,tud->tkd", tiles, picked, precision=lax.Precision.HIGHEST)
        summed = jnp.dot(
            item_pick, products.reshape(tile_count, -1), precision=lax.Precision.HIGHEST
        )
        partial_items = summed.reshape(item_blocks * tile_size, emb_width)
        users_now = (
            lax.psum_scatter(partial_users, "ia", scatter_dimension=0, tiled=True) * norm_user
        )
        if layer_index + 1 < LAYERS:
            gathered_users = lax.all_gather(users_now * norm_user, "ia", axis=0, tiled=True)
        items_now = (
            lax.psum_scatter(partial_items, "au", scatter_dimension=0, tiled=True) * norm_item
        )
        user_total = user_total + users_now
        item_total = item_total + items_now
    return (user_total / (LAYERS + 1.0), item_total / (LAYERS + 1.0))


def solution(mesh):
    in_specs = (
        P(("au", "ia"), None),
        P(("ia", "au"), None),
        P(("au", "ia")),
        P(("ia", "au")),
        P(("au", "ia"), None, None),
        P(("au", "ia")),
        P(("au", "ia")),
        P(("au", "ia")),
    )
    out_specs = (P(("au", "ia"), None), P(("ia", "au"), None))
    return jax.shard_map(
        per_device, mesh=mesh, in_specs=in_specs, out_specs=out_specs, check_vma=False
    )
```

profile of v0, /device:TPU:1, one launch (start us, length us, event | category | flops | bytes accessed | tf_op | source)
XLA Modules:
  0.0 558.9 jit_solution(12804511916847766787)
XLA Ops:
  7.2 0.7 convert_rsqrt_fusion
  7.9 1.8 broadcast_multiply_fusion
  11.1 40.5 %all-gather.7.cloned.1.call-done = f32[4096,128]{1,0:T(8,128)} async-done(((f32[512,128]{1,0:T(8,128)}), f32[4096,128]{1,0:T(8,128)}) %all-gather.7.cloned.1.call-update) | async-done | bytes 2097168 | tf_op jit(solution)/shard_map/all_gather | solution.py:34
  51.6 5.9 %gather_fusion.1 = f32[128,128,128]{2,1,0:T(8,128)} fusion(f32[32,128,128]{2,1,0:T(8,128)} %bitcast.32, s32[1024]{0:T(1024)S(1)} %pad_clamp_fusion), kind=kCustom, calls=%fused_computation.1 | custom fusion | bytes 16777728 | tf_op jit(solution)/shard_map/gather | solution.py:47
  57.5 19.0 %convolution_bitcast_fusion.2 = f32[128,128,128]{1,2,0:T(8,128)} fusion(f32[128,128,128]{2,1,0:T(8,128)} %gather_fusion.1, f32[128,128,128]{2,1,0:T(8,128)} %param.12), kind=kOutput, calls=%fused_computation.6 | convolution fusion | flops 3221225472 | bytes 25165824 | tf_op jit(solution)/shard_map/tuk,tud->tkd/dot_general | solution.py:48
  76.5 9.4 %copy.13 = f32[128,128,128]{0,2,1:T(8,128)} copy(f32[128,128,128]{1,2,0:T(8,128)} %convolution_bitcast_fusion.2) | data formatting | bytes 16777216 | tf_op jit(solution)/shard_map/tuk,tud->tkd/dot_general | solution.py:48
  86.0 10.8 %fusion.2 = f32[32,16384]{1,0:T(8,128)S(1)} fusion(f32[128,16384]{0,1:T(8,128)} %bitcast.35, s32[128]{0:T(128)S(1)} %copy-done.4, f32[128]{0:T(128)S(1)} %compare_convert_fusion), kind=kOutput, calls=%fused_computation.16 | convolution fusion | flops 805314560 | bytes 10486784 | tf_op jit(solution)/shard_map/dot_general | solution.py:49
  96.7 1.5 reshape.54
  98.3 87.1 %reduce-scatter.7.cloned.1.call-done = f32[128,128]{1,0:T(8,128)} async-done(((f32[4096,128]{1,0:T(8,128)}), f32[128,128]{1,0:T(8,128)}) %reduce-scatter.7.cloned.1.call-update) | async-done | bytes 65552 | tf_op jit(solution)/shard_map/reduce_scatter | solution.py:59
  185.5 1.6 broadcast_multiply_fusion.1
  187.9 51.1 %all-gather.9.cloned.1.call-done = f32[4096,128]{1,0:T(8,128)} async-done(((f32[128,128]{1,0:T(8,128)}), f32[4096,128]{1,0:T(8,128)}) %all-gather.9.cloned.1.call-update) | async-done | bytes 2097168 | tf_op jit(solution)/shard_map/all_gather | solution.py:38
  238.9 5.9 %gather_fusion.2 = f32[128,128,128]{2,1,0:T(8,128)} fusion(f32[32,128,128]{2,1,0:T(8,128)} %bitcast.31, s32[1024]{0:T(1024)S(1)} %pad_clamp_fusion.1), kind=kCustom, calls=%fused_computation.2 | custom fusion | bytes 16777728 | tf_op jit(solution)/shard_map/gather | solution.py:39
  244.8 19.0 %convolution_bitcast_fusion.1 = f32[128,128,128]{1,2,0:T(8,128)} fusion(f32[128,128,128]{2,1,0:T(8,128)} %gather_fusion.2, f32[128,128,128]{2,1,0:T(8,128)} %param.12), kind=kOutput, calls=%fused_computation.5 | convolution fusion | flops 3221225472 | bytes 25165824 | tf_op jit(solution)/shard_map/tuk,tkd->tud/dot_general | solution.py:40
  263.8 9.4 %copy.15 = f32[128,128,128]{0,2,1:T(8,128)} copy(f32[128,128,128]{1,2,0:T(8,128)} %convolution_bitcast_fusion.1) | data formatting | bytes 16777216 | tf_op jit(solution)/shard_map/tuk,tkd->tud/dot_general | solution.py:40
  273.3 10.7 %fusion.4 = f32[32,16384]{1,0:T(8,128)S(1)} fusion(f32[128,16384]{0,1:T(8,128)} %bitcast.36, f32[128]{0:T(128)S(1)} %compare_convert_fusion, s32[128]{0:T(128)S(1)} %copy-done.3), kind=kOutput, calls=%fused_computation.18 | convolution fusion | flops 805314560 | bytes 10486784 | tf_op jit(solution)/shard_map/dot_general | solution.py:43
  284.0 1.5 reshape.57
  285.8 4.3 all-gather.5.cloned.1.call-done
  290.1 5.9 %gather_fusion = f32[128,128,128]{2,1,0:T(8,128)} fusion(f32[32,128,128]{2,1,0:T(8,128)} %bitcast.30, s32[1024]{0:T(1024)S(1)} %pad_clamp_fusion.1), kind=kCustom, calls=%fused_computation | custom fusion | bytes 16777728 | tf_op jit(solution)/shard_map/gather | solution.py:39
  296.0 19.0 %convolution_bitcast_fusion.3 = f32[128,128,128]{1,2,0:T(8,128)} fusion(f32[128,128,128]{2,1,0:T(8,128)} %gather_fusion, f32[128,128,128]{2,1,0:T(8,128)} %param.12), kind=kOutput, calls=%fused_computation.7 | convolution fusion | flops 3221225472 | bytes 25165824 | tf_op jit(solution)/shard_map/tuk,tkd->tud/dot_general | solution.py:40
  315.0 9.5 %copy.11 = f32[128,128,128]{0,2,1:T(8,128)} copy(f32[128,128,128]{1,2,0:T(8,128)} %convolution_bitcast_fusion.3) | data formatting | bytes 16777216 | tf_op jit(solution)/shard_map/tuk,tkd->tud/dot_general | solution.py:40
  324.5 10.8 %fusion.6 = f32[32,16384]{1,0:T(8,128)S(1)} fusion(f32[128,16384]{0,1:T(8,128)} %bitcast.37, f32[128]{0:T(128)S(1)} %compare_convert_fusion, s32[128]{0:T(128)S(1)} %copy-done.3), kind=kOutput, calls=%fused_computation.20 | convolution fusion | flops 805314560 | bytes 10486784 | tf_op jit(solution)/shard_map/dot_general | solution.py:43
  335.2 1.5 reshape.51
  336.9 36.9 %reduce-scatter.5.cloned.1.call-done = f32[512,128]{1,0:T(8,128)} async-done(((f32[4096,128]{1,0:T(8,128)}), f32[512,128]{1,0:T(8,128)}) %reduce-scatter.5.cloned.1.call-update) | async-done | bytes 262160 | tf_op jit(solution)/shard_map/reduce_scatter | solution.py:54
  373.8 2.0 multiply_multiply_fusion
  376.1 40.2 %all-gather.11.cloned.1.call-done = f32[4096,128]{1,0:T(8,128)} async-done(((f32[512,128]{1,0:T(8,128)}), f32[4096,128]{1,0:T(8,128)}) %all-gather.11.cloned.1.call-update) | async-done | bytes 2097168 | tf_op jit(solution)/shard_map/all_gather | solution.py:57
  416.3 5.9 %gather_fusion.3 = f32[128,128,128]{2,1,0:T(8,128)} fusion(f32[32,128,128]{2,1,0:T(8,128)} %bitcast.33, s32[1024]{0:T(1024)S(1)} %pad_clamp_fusion), kind=kCustom, calls=%fused_computation.3 | custom fusion | bytes 16777728 | tf_op jit(solution)/shard_map/gather | solution.py:47
  422.2 19.0 %convolution_bitcast_fusion = f32[128,128,128]{1,2,0:T(8,128)} fusion(f32[128,128,128]{2,1,0:T(8,128)} %gather_fusion.3, f32[128,128,128]{2,1,0:T(8,128)} %param.12), kind=kOutput, calls=%fused_computation.4 | convolution fusion | flops 3221225472 | bytes 25165824 | tf_op jit(solution)/shard_map/tuk,tud->tkd/dot_general | solution.py:48
  441.2 9.4 %copy.17 = f32[128,128,128]{0,2,1:T(8,128)} copy(f32[128,128,128]{1,2,0:T(8,128)} %convolution_bitcast_fusion) | data formatting | bytes 16777216 | tf_op jit(solution)/shard_map/tuk,tud->tkd/dot_general | solution.py:48
  450.6 10.7 %fusion = f32[32,16384]{1,0:T(8,128)S(1)} fusion(f32[128,16384]{0,1:T(8,128)} %bitcast.34, s32[128]{0:T(128)S(1)} %copy-done.4, f32[128]{0:T(128)S(1)} %compare_convert_fusion), kind=kOutput, calls=%fused_computation.14 | convolution fusion | flops 805314560 | bytes 10486784 | tf_op jit(solution)/shard_map/dot_general | solution.py:49
  461.4 1.5 reshape.60
  462.9 87.2 %reduce-scatter.11.cloned.1.call-done = f32[128,128]{1,0:T(8,128)} async-done(((f32[4096,128]{1,0:T(8,128)}), f32[128,128]{1,0:T(8,128)}) %reduce-scatter.11.cloned.1.call-update) | async-done | bytes 65552 | tf_op jit(solution)/shard_map/reduce_scatter | solution.py:59
  550.1 1.6 add_multiply_fusion.1
  (35 shorter events, 2.3 us)
Async XLA Ops:
  7.2 44.4 %all-gather.7.cloned.1.call-start = ((), (), s32[]{:S(2)}) async-start(), calls=%async_computation.6 | async-start | bytes 2359296 | tf_op jit(solution)/shard_map/all_gather | solution.py:34
  9.7 175.7 %reduce-scatter.7.cloned.1.call-start = ((), (), s32[]{:S(2)}) async-start(), calls=%async_computation.7 | async-start | bytes 2162688 | tf_op jit(solution)/shard_map/reduce_scatter | solution.py:59
  76.5 9.4 %copy-start.4 = (s32[128]{0:T(128)S(1)}, s32[128]{0:T(128)}, u32[]{:S(2)}) copy-start(s32[128]{0:T(128)} %param.14) | copy-start | bytes 1540
  86.0 12.4 %copy-start.5 = (s32[128]{0:T(128)S(1)}, s32[128]{0:T(128)}, u32[]{:S(2)}) copy-start(s32[128]{0:T(128)} %param.11) | copy-start | bytes 1540
  86.0 99.5 %copy-start.1 = (f32[128,128]{1,0:T(8,128)S(1)}, f32[128,128]{1,0:T(8,128)}, u32[]{:S(2)}) copy-start(f32[128,128]{1,0:T(8,128)} %param.9) | copy-start | bytes 196612
  98.3 140.7 %all-gather.9.cloned.1.call-start = ((), (), s32[]{:S(2)}) async-start(), calls=%async_computation.8 | async-start | bytes 2162688 | tf_op jit(solution)/shard_map/all_gather | solution.py:38
  187.1 103.0 %all-gather.5.cloned.1.call-start = ((), (), s32[]{:S(2)}) async-start(), calls=%async_computation.4 | async-start | bytes 2162688 | tf_op jit(solution)/shard_map/all_gather | solution.py:38
  187.6 149.2 %reduce-scatter.9.cloned.1.call-start = ((), (), s32[]{:S(2)}) async-start(), calls=%async_computation.9 | async-start | bytes 2359296 | tf_op jit(solution)/shard_map/reduce_scatter | solution.py:54
  263.8 9.4 %copy-start.3 = (s32[128]{0:T(128)S(1)}, s32[128]{0:T(128)}, u32[]{:S(2)}) copy-start(s32[128]{0:T(128)} %param.13) | copy-start | bytes 1540
  285.6 88.2 %reduce-scatter.5.cloned.1.call-start = ((), (), s32[]{:S(2)}) async-start(), calls=%async_computation.5 | async-start | bytes 2359296 | tf_op jit(solution)/shard_map/reduce_scatter | solution.py:54
  324.5 49.3 %copy-start = (f32[512,128]{1,0:T(8,128)S(1)}, f32[512,128]{1,0:T(8,128)}, u32[]{:S(2)}) copy-start(f32[512,128]{1,0:T(8,128)} %param.8) | copy-start | bytes 786436
  336.8 79.5 %all-gather.11.cloned.1.call-start = ((), (), s32[]{:S(2)}) async-start(), calls=%async_computation.10 | async-start | bytes 2359296 | tf_op jit(solution)/shard_map/all_gather | solution.py:57
  375.8 174.3 %reduce-scatter.11.cloned.1.call-start = ((), (), s32[]{:S(2)}) async-start(), calls=%async_computation.11 | async-start | bytes 2162688 | tf_op jit(solution)/shard_map/reduce_scatter | solution.py:59
  450.6 99.5 %copy-start.2 = (f32[128,128]{1,0:T(8,128)S(1)}, f32[128,128]{1,0:T(8,128)}, u32[]{:S(2)}) copy-start(f32[128,128]{1,0:T(8,128)} %reduce-scatter.7.cloned.1.call-done) | copy-start | bytes 196612
Sparse Core Ops, SparseCore 0:
  10.4 41.1 all-gather.6
  98.4 87.0 reduce-scatter.6
  188.6 50.3 all-gather.8
  241.9 48.1 all-gather.4
  292.5 36.8 reduce-scatter.8
  336.9 36.8 reduce-scatter.4
  375.9 40.3 all-gather.10
  463.0 87.0 reduce-scatter.10
where the time goes:
time: 569 us; the launch traced here: 559 us
  waiting for transfers between devices  348 us (61%)
  matrix products  119 us (21%)
  local copies, waits for them, and re-layouts  67.5 us (12%)
  between operations  15.3 us (3%)
  other arithmetic  8.25 us (1%)
    reduce_scatter x2, waiting for transfers between devices, per_device(): lax.psum_scatter(partial_items, 'au', scatter_dimension=0, tiled=True)  174 us
    all_gather x2, waiting for transfers between devices, per_device(): lax.all_gather(items_now * norm_item, 'au', axis=0, tiled=True)  55.3 us
    all_gather x1, waiting for transfers between devices, per_device(): lax.all_gather(user_emb * norm_user, 'ia', axis=0, tiled=True)  40.5 us
    all_gather x1, waiting for transfers between devices, per_device(): lax.all_gather(users_now * norm_user, 'ia', axis=0, tiled=True)  40.2 us
    dot_general x2, matrix products, per_device(): jnp.einsum('tuk,tud->tkd', tiles, picked, precision=lax.Precision.HIGHEST)  38 us
    dot_general x2, matrix products, per_device(): jnp.einsum('tuk,tkd->tud', tiles, toward_picked, precision=lax.Precision....  38 us
    reduce_scatter x2, waiting for transfers between devices, per_device(): lax.psum_scatter(partial_users, 'ia', scatter_dimension=0, tiled=True)  36.9 us
    dot_general x2, matrix products, per_device(): jnp.dot(item_pick, products.reshape(tile_count, -1), precision=lax.Precis...  21.5 us
  transfers between devices with their start and end apart: 8, of which 7 were waited for; matrix products, arithmetic and copies ran while one was open for 17% of the time, Pallas kernels for 0%

commit v1 on v0

v1 whole, which is shorter than its diff:
```python
import functools
import heapq

import jax
import jax.numpy as jnp
from jax import lax
from jax.experimental import pallas as pl
from jax.experimental.pallas import tpu as pltpu
from jax.sharding import PartitionSpec as P

MESH = pl.DeviceIdType.MESH
LAYERS = 2
T = 128
NZ = 8
NX, NY = 4, 4
CHIPS = NX * NY
AU = 2 * CHIPS
UB = 32
IB = 32
SLOTS = 128
PER_Z = UB // NZ
RC = 4
ROWS = PER_Z * T // (2 * RC)
OFFSETS = sorted(
    ((dx, dy) for dx in range(NX) for dy in range(NY)),
    key=lambda o: -(min(o[0], NX - o[0]) + min(o[1], NY - o[1])),
)
PEERS = OFFSETS[:-1]
AG_RIGHT = [(s, c) for s in range(NZ // 2) for c in range(PER_Z) if s < NZ // 2 - 1 or c < PER_Z // 2]
AG_LEFT = [(s, c) for s in range(NZ // 2) for c in range(PER_Z) if s < NZ // 2 - 1 or c >= PER_Z // 2]
PIECE = 16
UNROLL = 4


def halves(value):
    high = value.astype(jnp.bfloat16)
    low = (value - high.astype(jnp.float32)).astype(jnp.bfloat16)
    return jnp.concatenate([high, low], axis=1)


def column(row):
    return jnp.transpose(jnp.broadcast_to(row, (T, T)))


def merge(chains):
    heap = []
    for at, (start, gen) in enumerate(chains):
        heap.append((start, at, gen))
    heapq.heapify(heap)
    while heap:
        when, at, gen = heapq.heappop(heap)
        step = next(gen, None)
        if step is not None:
            heapq.heappush(heap, (when + step, at, gen))


class Place:
    def __init__(self):
        self.au = lax.axis_index("au")
        self.z = lax.axis_index("ia")
        self.core = lax.rem(self.au, 2)
        self.x = lax.rem(self.au // 2, NX)
        self.y = self.au // (2 * NX)
        self.partner = self.au + 1 - 2 * self.core

    def chip(self, dx, dy):
        return lax.rem(self.y + dy, NY) * NX + lax.rem(self.x + dx, NX)

    def ring(self, step):
        return lax.rem(self.z + NZ + step, NZ)


class GatherZ:
    def __init__(self, me, buf, sems, on_chunk):
        self.me, self.buf, self.sems, self.on_chunk = me, buf, sems, on_chunk
        self.plans = (AG_RIGHT, AG_LEFT)

    def copy(self, way, k, received=False):
        me = self.me
        s, c = self.plans[way][k]
        sign = 1 if way == 0 else -1
        block = me.ring(-sign * (s + (1 if received else 0)))
        ref = self.buf.at[block, pl.ds(c * T, T)]
        return (
            pltpu.make_async_remote_copy(
                src_ref=ref,
                dst_ref=ref,
                send_sem=self.sems.at[2 * way, k],
                recv_sem=self.sems.at[2 * way + 1, k],
                device_id=(me.au, me.ring(sign)),
                device_id_type=MESH,
            ),
            block,
            c,
        )

    def start_own(self, c):
        for way in range(2):
            self.copy(way, self.plans[way].index((0, c)))[0].start()

    def run(self, dt):
        order = []
        for k in range(len(AG_RIGHT)):
            order += [(0, k), (1, k)]
        for way, k in order:
            yield dt / 2
            s, c = self.plans[way][k]
            copy, block, c = self.copy(way, k, received=True)
            copy.wait_recv()
            if (s + 1, c) in self.plans[way]:
                self.copy(way, self.plans[way].index((s + 1, c)))[0].start()
            self.on_chunk(block, c)

    def finish(self):
        for way in range(2):
            for k in range(len(self.plans[way])):
                self.copy(way, k)[0].wait_send()


class ScatterZ:
    def __init__(self, me, q, land, sems, on_final):
        self.me, self.q, self.land, self.sems, self.on_final = me, q, land, sems, on_final

    def part(self, block, way, c):
        rows = way * RC * ROWS + c * ROWS
        return self.q.at[block * PER_Z + rows // T, pl.ds(rows % T, ROWS)]

    def copy(self, way, s, c):
        me = self.me
        sign = 1 if way == 0 else -1
        if s == 0:
            src = self.part(me.ring(-sign), way, c)
        else:
            src = self.land.at[way, s - 1, c]
        return pltpu.make_async_remote_copy(
            src_ref=src,
            dst_ref=self.land.at[way, s, c],
            send_sem=self.sems.at[2 * way, s * RC + c],
            recv_sem=self.sems.at[2 * way + 1, s * RC + c],
            device_id=(me.au, me.ring(sign)),
            device_id_type=MESH,
        )

    def start(self):
        for c in range(RC):
            for way in range(2):
                self.copy(way, 0, c).start()

    def run(self, dt):
        me = self.me
        for s in range(NZ - 1):
            for c in range(RC):
                for way in range(2):
                    yield dt / 2
                    sign = 1 if way == 0 else -1
                    self.copy(way, s, c).wait_recv()
                    mine = self.part(me.ring(-sign * (s + 2)), way, c)
                    value = self.land[way, s, c] + mine[...]
                    if s < NZ - 2:
                        self.land[way, s, c] = value
                        self.copy(way, s + 1, c).start()
                    else:
                        self.on_final(way * RC * ROWS + c * ROWS, value)

    def finish(self):
        for s in range(NZ - 1):
            for c in range(RC):
                for way in range(2):
                    self.copy(way, s, c).wait_send()


class GatherPlane:
    def __init__(self, me, buf, sems, on_block):
        self.me, self.buf, self.sems, self.on_block = me, buf, sems, on_block

    def send(self, k):
        me = self.me
        dx, dy = PEERS[k]
        ref = self.buf.at[me.au]
        return pltpu.make_async_remote_copy(
            src_ref=ref, dst_ref=ref,
            send_sem=self.sems.at[0, k], recv_sem=self.sems.at[1, k],
            device_id=(2 * me.chip(dx, dy) + me.core, me.z), device_id_type=MESH,
        )

    def source(self, k):
        dx, dy = OFFSETS[k]
        return 2 * self.me.chip(NX - dx, NY - dy)

    def landed(self, k):
        me = self.me
        dx, dy = PEERS[k]
        ref = self.buf.at[self.source(k) + me.core]
        return pltpu.make_async_remote_copy(
            src_ref=ref, dst_ref=ref,
            send_sem=self.sems.at[0, k], recv_sem=self.sems.at[1, k],
            device_id=(2 * me.chip(dx, dy) + me.core, me.z), device_id_type=MESH,
        )

    def across(self, k, received=False):
        me = self.me
        side = 1 - me.core if received else me.core
        ref = self.buf.at[self.source(k) + side]
        return pltpu.make_async_remote_copy(
            src_ref=ref, dst_ref=ref,
            send_sem=self.sems.at[2, k], recv_sem=self.sems.at[3, k],
            device_id=(me.partner, me.z), device_id_type=MESH,
        )

    def start(self):
        for k in range(len(PEERS)):
            self.send(k).start()
        self.across(CHIPS - 1).start()

    def run(self, dt, dt_across):
        me = self.me
        self.on_block(me.au)
        for k in reversed(range(len(PEERS))):
            yield dt
            self.landed(k).wait_recv()
            self.across(k).start()
            self.on_block(self.source(k) + me.core)
        for k in reversed(range(CHIPS)):
            yield dt_across
            self.across(k, received=True).wait_recv()
            self.on_block(self.source(k) + 1 - me.core)

    def finish(self):
        for k in range(len(PEERS)):
            self.send(k).wait_send()
        for k in range(CHIPS):
            self.across(k).wait_send()


class ScatterPlane:
    def __init__(self, me, p, pair, home, sems, on_final):
        self.me, self.p, self.pair, self.home = me, p, pair, home
        self.sems, self.on_final = sems, on_final

    def across(self, k):
        me = self.me
        dx, dy = OFFSETS[k]
        return pltpu.make_async_remote_copy(
            src_ref=self.p.at[2 * me.chip(dx, dy) + 1 - me.core], dst_ref=self.pair.at[k],
            send_sem=self.sems.at[0, k], recv_sem=self.sems.at[1, k],
            device_id=(me.partner, me.z), device_id_type=MESH,
        )

    def send(self, k):
        me = self.me
        dx, dy = PEERS[k]
        return pltpu.make_async_remote_copy(
            src_ref=self.pair.at[k], dst_ref=self.home.at[k],
            send_sem=self.sems.at[2, k], recv_sem=self.sems.at[3, k],
            device_id=(2 * me.chip(dx, dy) + me.core, me.z), device_id_type=MESH,
        )

    def start(self):
        for k in range(CHIPS):
            self.across(k).start()

    def run(self, dt_across, dt):
        me = self.me
        for k in range(CHIPS):
            yield dt_across
            self.across(k).wait_recv()
            dx, dy = OFFSETS[k]
            self.pair[k] = self.pair[k] + self.p[2 * me.chip(dx, dy) + me.core]
            if k < len(PEERS):
                self.send(k).start()
        for k in reversed(range(len(PEERS))):
            yield dt
            self.send(k).wait_recv()
            self.pair[CHIPS - 1] = self.pair[CHIPS - 1] + self.home[k]
        self.on_final(self.pair[CHIPS - 1])

    def finish(self):
        for k in range(CHIPS):
            self.across(k).wait_send()
        for k in range(len(PEERS)):
            self.send(k).wait_send()


def kernel(
    table, user_emb, item_emb, user_degree, item_degree, tiles_hbm,
    user_out, item_out,
    tiles, run, ug, vg, u2, v2, q, p, land, pair, home, user_scale, item_scale,
    tile_sem, gz_sems, sz_sems, gp_sems, sp_sems,
):
    me = Place()
    load = pltpu.make_async_copy(tiles_hbm, tiles, tile_sem)
    load.start()

    barrier = pltpu.get_barrier_semaphore()
    greeted = [(me.au, me.ring(1)), (me.au, me.ring(-1)), (me.partner, me.z)]
    greeted += [(2 * me.chip(dx, dy) + me.core, me.z) for dx, dy in PEERS]
    for device in greeted:
        pl.semaphore_signal(barrier, inc=1, device_id=device, device_id_type=MESH)

    item_scale[...] = column(lax.rsqrt(item_degree[...].astype(jnp.float32)))
    vg[0, me.au] = item_emb[...] * item_scale[...]
    for c in range(PER_Z):
        rows = pl.ds(c * T, T)
        user_scale[rows] = column(lax.rsqrt(user_degree[c : c + 1].astype(jnp.float32)))
        ug[0, me.z, rows] = user_emb[rows] * user_scale[rows]
    user_out[...] = user_emb[...]
    item_out[...] = item_emb[...]
    run[0] = jnp.zeros((T, T), jnp.float32)
    pl.semaphore_wait(barrier, len(greeted))

    def user_chunk(layer):
        def take(block, c):
            u2[block * PER_Z + c] = halves(ug[layer, block, pl.ds(c * T, T)])
        return take

    def item_block(layer):
        def take(block):
            v2[block] = halves(vg[layer, block])
        return take

    gather_z = [GatherZ(me, ug.at[l], gz_sems.at[l], user_chunk(l)) for l in range(LAYERS)]
    gather_plane = [GatherPlane(me, vg.at[l], gp_sems.at[l], item_block(l)) for l in range(LAYERS)]

    def user_final(layer):
        last = layer + 1 == LAYERS
        def take(row, value):
            rows = pl.ds(row, ROWS)
            scale = user_scale[rows]
            now = value * scale
            total = user_out[rows] + now
            user_out[rows] = total * (1.0 / (LAYERS + 1.0)) if last else total
            if not last:
                ug[layer + 1, me.z, rows] = now * scale
                if (row + ROWS) % T == 0:
                    gather_z[layer + 1].start_own(row // T)
                    user_chunk(layer + 1)(me.z, row // T)
        return take

    def item_final(layer):
        last = layer + 1 == LAYERS
        def take(value):
            now = value * item_scale[...]
            total = item_out[...] + now
            item_out[...] = total * (1.0 / (LAYERS + 1.0)) if last else total
            if not last:
                vg[layer + 1, me.au] = now * item_scale[...]
                gather_plane[layer + 1].start()
        return take

    scatter_z = [ScatterZ(me, q.at[l], land.at[l], sz_sems.at[l], user_final(l)) for l in range(LAYERS)]
    scatter_plane = [
        ScatterPlane(me, p.at[l], pair.at[l], home.at[l], sp_sems.at[l], item_final(l)) for l in range(LAYERS)
    ]

    def products(kind, source, out, dt):
        base = 4 * kind
        def step(at, carry):
            acc = run[at * UNROLL]
            for i in range(UNROLL):
                slot = at * UNROLL + i
                w = tiles[table[base, slot]]
                if kind == 1:
                    w = jnp.transpose(w)
                rows = source[table[base + 1, slot]]
                wide = jnp.dot(
                    halves(w), jnp.concatenate([rows, rows], axis=0), preferred_element_type=jnp.float32
                )
                keep = table[base + 2, slot].astype(jnp.float32)
                acc = acc * keep + (wide[:, :T] + wide[:, T:])
                run[slot + 1] = acc
            return carry
        per = PIECE // UNROLL
        for piece in range(SLOTS // PIECE):
            yield dt
            lax.fori_loop(piece * per, (piece + 1) * per, step, 0)
        def pick(block, carry):
            out[block] = run[table[base + 3, block]]
            return carry
        yield dt
        lax.fori_loop(0, UB, pick, 0)

    for c in range(PER_Z):
        gather_z[0].start_own(c)
        user_chunk(0)(me.z, c)
    gather_plane[0].start()

    def items_then_products(layer, first):
        yield 1e-3
        yield from first
        yield from gather_plane[layer].run(0.9, 0.1)
        if layer == 0:
            load.wait()
        yield from products(0, v2, q.at[layer], 0.35)
        scatter_z[layer].start()

    def empty():
        return
        yield

    merge([(0.0, items_then_products(0, empty())), (1.0, gather_z[0].run(1.4))])

    def plane_chain():
        yield from products(1, u2, p.at[0], 0.35)
        scatter_plane[0].start()
        yield from items_then_products(1, scatter_plane[0].run(0.3, 0.7))

    def z_chain():
        yield from scatter_z[0].run(0.7)
        yield from gather_z[1].run(1.4)

    merge([(0.0, plane_chain()), (1.0, z_chain())])

    def last_plane():
        yield from products(1, u2, p.at[1], 0.35)
        scatter_plane[1].start()
        yield from scatter_plane[1].run(0.3, 0.7)

    merge([(0.0, last_plane()), (1.0, scatter_z[1].run(0.7))])

    for layer in range(LAYERS):
        for chain in (gather_z, gather_plane, scatter_z, scatter_plane):
            chain[layer].finish()


def sorted_slots(keys, others):
    slots = jnp.arange(SLOTS, dtype=jnp.int32)
    before = (keys[:, None] < keys[None, :]) | (
        (keys[:, None] == keys[None, :]) & (slots[:, None] < slots[None, :])
    )
    place = jnp.sum(before.astype(jnp.int32), axis=0)
    hit = (place[:, None] == slots[None, :]).astype(jnp.int32)
    order = jnp.sum(hit * slots[:, None], axis=0)
    block = jnp.sum(hit * others[:, None], axis=0)
    key_sorted = jnp.sum(hit * keys[:, None], axis=0)
    first = jnp.sum((keys[:, None] < key_sorted[None, :]).astype(jnp.int32), axis=0) == slots
    upto = jnp.sum((keys[:, None] <= slots[None, :]).astype(jnp.int32), axis=0)
    any_of = jnp.sum((keys[:, None] == slots[None, :]).astype(jnp.int32), axis=0) > 0
    return [order, block, 1 - first.astype(jnp.int32), jnp.where(any_of, upto, 0)]


def per_device(
    user_emb, item_emb, user_degree, item_degree, tiles, tile_user_block, tile_item_block, live_tiles
):
    live = jnp.arange(SLOTS, dtype=jnp.int32) < live_tiles[0]
    by_user = sorted_slots(jnp.where(live, tile_user_block, UB), tile_item_block)
    by_item = sorted_slots(jnp.where(live, tile_item_block, IB), tile_user_block)
    table = jnp.stack(by_user + by_item)
    f32 = jnp.float32
    vmem = pl.BlockSpec(memory_space=pltpu.VMEM)
    dma = pltpu.SemaphoreType.DMA
    return pl.pallas_call(
        kernel,
        out_shape=[
            jax.ShapeDtypeStruct((PER_Z * T, T), f32),
            jax.ShapeDtypeStruct((T, T), f32),
        ],
        in_specs=[pl.BlockSpec(memory_space=pltpu.SMEM)] + [vmem] * 4 + [pl.BlockSpec(memory_space=pl.ANY)],
        out_specs=[vmem, vmem],
        scratch_shapes=[
            pltpu.VMEM((SLOTS, T, T), f32),
            pltpu.VMEM((SLOTS + 1, T, T), f32),
            pltpu.VMEM((LAYERS, NZ, PER_Z * T, T), f32),
            pltpu.VMEM((LAYERS, AU, T, T), f32),
            pltpu.VMEM((UB, T, 2 * T), jnp.bfloat16),
            pltpu.VMEM((IB, T, 2 * T), jnp.bfloat16),
            pltpu.VMEM((LAYERS, UB, T, T), f32),
            pltpu.VMEM((LAYERS, IB, T, T), f32),
            pltpu.VMEM((LAYERS, 2, NZ - 1, RC, ROWS, T), f32),
            pltpu.VMEM((LAYERS, CHIPS, T, T), f32),
            pltpu.VMEM((LAYERS, CHIPS - 1, T, T), f32),
            pltpu.VMEM((PER_Z * T, T), f32),
            pltpu.VMEM((T, T), f32),
            dma,
            dma((LAYERS, 4, len(AG_RIGHT))),
            dma((LAYERS, 4, (NZ - 1) * RC)),
            dma((LAYERS, 4, CHIPS)),
            dma((LAYERS, 4, CHIPS)),
        ],
        compiler_params=pltpu.CompilerParams(
            collective_id=0, has_side_effects=True, vmem_limit_bytes=62 << 20
        ),
    )(
        table, user_emb, item_emb, user_degree.reshape(PER_Z, T), item_degree.reshape(1, T), tiles
    )


def solution(mesh):
    in_specs = (
        P(("au", "ia"), None),
        P(("ia", "au"), None),
        P(("au", "ia")),
        P(("ia", "au")),
        P(("au", "ia"), None, None),
        P(("au", "ia")),
        P(("au", "ia")),
        P(("au", "ia")),
    )
    out_specs = (P(("au", "ia"), None), P(("ia", "au"), None))
    return jax.shard_map(
        per_device, mesh=mesh, in_specs=in_specs, out_specs=out_specs, check_vma=False
    )
```

time: 569 us -> 175 us (0.31); the launches traced: 559 us -> 174 us
  waiting for transfers between devices: 348 us -> 0 us
  Pallas kernels: 0 us -> 166 us
  matrix products: 119 us -> 0 us
  local copies, waits for them, and re-layouts: 67.5 us -> 3.76 us
  between operations: 15.3 us -> 1.32 us
    reduce_scatter x4 -> x0, waiting for transfers between devices: 211 us -> none  [the longest x2 174 us: per_device(): lax.psum_scatter(partial_items, 'au', scatter_dimension=0, tiled=True)]
    pallas_call x0 -> x1, Pallas kernels: none -> 166 us  [per_device(): pl.pallas_call(kernel, out_shape=[jax.ShapeDtypeStruct((PER_Z * T, T), f3...]
    all_gather x4 -> x0, waiting for transfers between devices: 136 us -> none  [the longest x2 55.3 us: per_device(): lax.all_gather(items_now * norm_item, 'au', axis=0, tiled=True)]
    dot_general x8 -> x0, matrix products: 119 us -> none  [the longest x2 38 us: per_device(): jnp.einsum('tuk,tud->tkd', tiles, picked, precision=lax.Precision.HIGHEST)]
    dot_general x4 -> x0, local copies, waits for them, and re-layouts: 37.8 us -> none  [the longest x2 18.9 us: per_device(): jnp.einsum('tuk,tkd->tud', tiles, toward_picked, precision=lax.Precision....]
    gather x4 -> x0, local copies, waits for them, and re-layouts: 23.6 us -> none  [the longest x2 11.8 us: per_device(): gathered_items.reshape(item_blocks, tile_size, emb_width)[tile_item_block]]
    reshape x4 -> x0, local copies, waits for them, and re-layouts: 6.06 us -> none  [the longest x2 3.03 us: per_device(): partial_users = toward_summed.reshape(user_blocks * tile_size, emb_width)]
  transfers between devices with their start and end apart: 8 -> 0, of which waited for: 7 -> 0; matrix products, arithmetic and copies ran while one was open for 17% -> 0% of each run, Pallas kernels for 0% -> 0%
where the time goes in v1:
time: 175 us; the launch traced here: 174 us
  Pallas kernels  166 us (95%)
  local copies, waits for them, and re-layouts  3.76 us (2%)
  other arithmetic  2.68 us (2%)
    pallas_call x1, Pallas kernels, per_device(): pl.pallas_call(kernel, out_shape=[jax.ShapeDtypeStruct((PER_Z * T, T), f3...  166 us

profile of v1, /device:TPU:1, one launch (start us, length us, event | category | flops | bytes accessed | tf_op | source)
XLA Modules:
  0.0 173.7 jit_solution(17503932800949693365)
XLA Ops:
  1.3 0.7 compare_select_fusion.2
  2.0 0.1 convert_reduce_fusion.3
  2.1 0.1 convert_reduce_fusion.7
  2.2 0.8 convert_reduce_fusion.5
  3.0 0.1 convert_reduce_fusion.6
  3.1 0.8 convert_reduce_fusion.1
  3.9 0.1 convert_reduce_fusion.2
  4.0 0.6 stack.23.table
  4.6 166.0 %shard_map.95 = (f32[512,128]{1,0:T(8,128)}, f32[128,128]{1,0:T(8,128)}) custom-call(s32[8,128]{1,0:T(8,128)} %stack.23.table, f32[512,128]{1,0:T(8,128)} %user_emb.1, f32[128,128]{1,0:T(8,128)} %item_emb.1, s32[4,128]{1,0:T(4,128)} %bitcast.16, s32[1,128]{1,0:T(1,128)} %bitcast.21, f32[128,128,128]{2,1,0:T(8,128)} %tiles_hbm.1), custom_call_target="tpu_custom_call" | custom-call | tf_op jit(solution)/shard_map/pallas_call | solution.py:451
  170.6 1.7 copy.13
  172.3 1.5 copy.14
  (4 shorter events, 0.0 us)

commit v2 on v1

--- a/solution.py
+++ b/solution.py
@@ -28,8 +28,8 @@
 PEERS = OFFSETS[:-1]
 AG_RIGHT = [(s, c) for s in range(NZ // 2) for c in range(PER_Z) if s < NZ // 2 - 1 or c < PER_Z // 2]
 AG_LEFT = [(s, c) for s in range(NZ // 2) for c in range(PER_Z) if s < NZ // 2 - 1 or c >= PER_Z // 2]
-PIECE = 16
-UNROLL = 4
+PIECE = 32
+UNROLL = 32
 
 
 def halves(value):
@@ -215,12 +215,13 @@
     def run(self, dt, dt_across):
         me = self.me
         self.on_block(me.au)
-        for k in reversed(range(len(PEERS))):
+        yield 2.0
+        for k in range(len(PEERS)):
             yield dt
             self.landed(k).wait_recv()
             self.across(k).start()
             self.on_block(self.source(k) + me.core)
-        for k in reversed(range(CHIPS)):
+        for k in [CHIPS - 1] + list(range(len(PEERS))):
             yield dt_across
             self.across(k, received=True).wait_recv()
             self.on_block(self.source(k) + 1 - me.core)
@@ -268,7 +269,7 @@
             self.pair[k] = self.pair[k] + self.p[2 * me.chip(dx, dy) + me.core]
             if k < len(PEERS):
                 self.send(k).start()
-        for k in reversed(range(len(PEERS))):
+        for k in range(len(PEERS)):
             yield dt
             self.send(k).wait_recv()
             self.pair[CHIPS - 1] = self.pair[CHIPS - 1] + self.home[k]
@@ -376,7 +377,7 @@
         def pick(block, carry):
             out[block] = run[table[base + 3, block]]
             return carry
-        yield dt
+        yield 0.4
         lax.fori_loop(0, UB, pick, 0)
 
     for c in range(PER_Z):
@@ -390,32 +391,32 @@
         yield from gather_plane[layer].run(0.9, 0.1)
         if layer == 0:
             load.wait()
-        yield from products(0, v2, q.at[layer], 0.35)
+        yield from products(0, v2, q.at[layer], 0.9)
         scatter_z[layer].start()
 
     def empty():
         return
         yield
 
-    merge([(0.0, items_then_products(0, empty())), (1.0, gather_z[0].run(1.4))])
+    merge([(0.0, items_then_products(0, empty())), (1.0, gather_z[0].run(1.6))])
 
     def plane_chain():
-        yield from products(1, u2, p.at[0], 0.35)
+        yield from products(1, u2, p.at[0], 0.9)
         scatter_plane[0].start()
         yield from items_then_products(1, scatter_plane[0].run(0.3, 0.7))
 
     def z_chain():
-        yield from scatter_z[0].run(0.7)
-        yield from gather_z[1].run(1.4)
+        yield from scatter_z[0].run(0.86)
+        yield from gather_z[1].run(1.6)
 
     merge([(0.0, plane_chain()), (1.0, z_chain())])
 
     def last_plane():
-        yield from products(1, u2, p.at[1], 0.35)
+        yield from products(1, u2, p.at[1], 0.9)
         scatter_plane[1].start()
         yield from scatter_plane[1].run(0.3, 0.7)
 
-    merge([(0.0, last_plane()), (1.0, scatter_z[1].run(0.7))])
+    merge([(0.0, last_plane()), (1.0, scatter_z[1].run(0.86))])
 
     for layer in range(LAYERS):
         for chain in (gather_z, gather_plane, scatter_z, scatter_plane):

time: 175 us -> 135 us (0.77)
  Pallas kernels: 166 us -> 127 us
    pallas_call x1, Pallas kernels: 166 us -> 127 us  [per_device(): pl.pallas_call(kernel, out_shape=[jax.ShapeDtypeStruct((PER_Z * T, T), f3...]
where the time goes in v2:
time: 135 us
  Pallas kernels  127 us (94%)
  local copies, waits for them, and re-layouts  3.76 us (3%)
  other arithmetic  2.68 us (2%)
    pallas_call x1, Pallas kernels, per_device(): pl.pallas_call(kernel, out_shape=[jax.ShapeDtypeStruct((PER_Z * T, T), f3...  127 us
    unnamed x2, local copies, waits for them, and re-layouts  3.14 us

profile of v2, /device:TPU:1, one launch (start us, length us, event | category | flops | bytes accessed | tf_op | source)
XLA Modules:
  0.0 134.6 jit_solution(9972449240445856038)
XLA Ops:
  1.3 0.7 compare_select_fusion.2
  2.0 0.1 convert_reduce_fusion.3
  2.1 0.1 convert_reduce_fusion.7
  2.2 0.8 convert_reduce_fusion.5
  3.0 0.1 convert_reduce_fusion.6
  3.1 0.8 convert_reduce_fusion.1
  3.9 0.1 convert_reduce_fusion.2
  4.0 0.6 stack.23.table
  4.6 126.8 %shard_map.95 = (f32[512,128]{1,0:T(8,128)}, f32[128,128]{1,0:T(8,128)}) custom-call(s32[8,128]{1,0:T(8,128)} %stack.23.table, f32[512,128]{1,0:T(8,128)} %user_emb.1, f32[128,128]{1,0:T(8,128)} %item_emb.1, s32[4,128]{1,0:T(4,128)} %bitcast.16, s32[1,128]{1,0:T(1,128)} %bitcast.21, f32[128,128,128]{2,1,0:T(8,128)} %tiles_hbm.1), custom_call_target="tpu_custom_call" | custom-call | tf_op jit(solution)/shard_map/pallas_call | solution.py:452
  131.4 1.7 %copy.13 = f32[512,128]{1,0:T(8,128)} copy(f32[512,128]{1,0:T(8,128)} %get-tuple-element.16) | data formatting | bytes 524288
  133.1 1.5 %copy.14 = f32[128,128]{1,0:T(8,128)} copy(f32[128,128]{1,0:T(8,128)} %get-tuple-element.17) | data formatting | bytes 131072
  (4 shorter events, 0.0 us)

commit v3 on v2

--- a/solution.py
+++ b/solution.py
@@ -398,7 +398,7 @@
         return
         yield
 
-    merge([(0.0, items_then_products(0, empty())), (1.0, gather_z[0].run(1.6))])
+    merge([(0.0, items_then_products(0, empty())), (1.0, gather_z[0].run(1.45))])
 
     def plane_chain():
         yield from products(1, u2, p.at[0], 0.9)
@@ -406,8 +406,8 @@
         yield from items_then_products(1, scatter_plane[0].run(0.3, 0.7))
 
     def z_chain():
-        yield from scatter_z[0].run(0.86)
-        yield from gather_z[1].run(1.6)
+        yield from scatter_z[0].run(0.72)
+        yield from gather_z[1].run(1.45)
 
     merge([(0.0, plane_chain()), (1.0, z_chain())])
 
@@ -416,7 +416,7 @@
         scatter_plane[1].start()
         yield from scatter_plane[1].run(0.3, 0.7)
 
-    merge([(0.0, last_plane()), (1.0, scatter_z[1].run(0.86))])
+    merge([(0.0, last_plane()), (1.0, scatter_z[1].run(0.72))])
 
     for layer in range(LAYERS):
         for chain in (gather_z, gather_plane, scatter_z, scatter_plane):

time: 135 us -> 132 us (0.978)
  Pallas kernels: 127 us -> 124 us
    pallas_call x1, Pallas kernels: 127 us -> 124 us  [per_device(): pl.pallas_call(kernel, out_shape=[jax.ShapeDtypeStruct((PER_Z * T, T), f3...]
where the time goes in v3:
time: 132 us
  Pallas kernels  124 us (94%)
  local copies, waits for them, and re-layouts  3.76 us (3%)
  other arithmetic  2.68 us (2%)
  between operations  1.32 us (1%)
    pallas_call x1, Pallas kernels, per_device(): pl.pallas_call(kernel, out_shape=[jax.ShapeDtypeStruct((PER_Z * T, T), f3...  124 us
    unnamed x2, local copies, waits for them, and re-layouts  3.14 us

profile of v3, /device:TPU:1, one launch (start us, length us, event | category | flops | bytes accessed | tf_op | source)
XLA Modules:
  0.0 131.8 jit_solution(8383956488784617561)
XLA Ops:
  1.3 0.7 compare_select_fusion.2
  2.0 0.1 convert_reduce_fusion.3
  2.1 0.1 convert_reduce_fusion.7
  2.2 0.8 convert_reduce_fusion.5
  3.0 0.1 convert_reduce_fusion.6
  3.1 0.8 convert_reduce_fusion.1
  3.9 0.1 convert_reduce_fusion.2
  4.0 0.6 stack.23.table
  4.6 124.0 %shard_map.95 = (f32[512,128]{1,0:T(8,128)}, f32[128,128]{1,0:T(8,128)}) custom-call(s32[8,128]{1,0:T(8,128)} %stack.23.table, f32[512,128]{1,0:T(8,128)} %user_emb.1, f32[128,128]{1,0:T(8,128)} %item_emb.1, s32[4,128]{1,0:T(4,128)} %bitcast.16, s32[1,128]{1,0:T(1,128)} %bitcast.21, f32[128,128,128]{2,1,0:T(8,128)} %tiles_hbm.1), custom_call_target="tpu_custom_call" | custom-call | tf_op jit(solution)/shard_map/pallas_call | solution.py:452
  128.7 1.7 %copy.13 = f32[512,128]{1,0:T(8,128)} copy(f32[512,128]{1,0:T(8,128)} %get-tuple-element.16) | data formatting | bytes 524288
  130.3 1.5 %copy.14 = f32[128,128]{1,0:T(8,128)} copy(f32[128,128]{1,0:T(8,128)} %get-tuple-element.17) | data formatting | bytes 131072
  (4 shorter events, 0.0 us)
